TPU v7x, 32 devices: a whole 2x2x4 slice. The times are simulated.
32 devices in a mesh: dp: 16 (over z, y, x), mp: 2 (over core).
Axes of the slice: x: 2, y: 2, z: 4, core: 2. Of those that a mesh axis runs over, the one named last changes fastest.
Arguments:
- tokens: bfloat16 [2, 512, 16, 768], P('mp', 'dp'), may hold values from -6 to 6
- cotangent: bfloat16 [2, 512, 16, 768], P('mp', 'dp'), may hold values from -6 to 6
- lengths: int32 [16], replicated, may hold values from 128 to 1024, as said below
- deal_order: int32 [16], replicated, may hold values from 0 to 15, as said below
- attn_in: bfloat16 [1, 3, 768, 768], P(None, None, 'dp', 'mp'), may hold values from -0.21875 to 0.21875
- attn_out: bfloat16 [1, 768, 768], P(None, 'mp', 'dp'), may hold values from -0.875 to 0.875
- ffn_in: bfloat16 [1, 768, 3072], P(None, 'dp', 'mp'), may hold values from -0.21875 to 0.21875
- ffn_out: bfloat16 [1, 3072, 768], P(None, 'mp', 'dp'), may hold values from -0.109375 to 0.109375
- attn_bias: bfloat16 [1, 2, 768], replicated, may hold values from -3 to 3
- ffn_bias: bfloat16 [1, 3072], replicated, may hold values from -3 to 3
- norm_gain: bfloat16 [1, 2, 768], replicated, may hold values from 0.5 to 1.5
- shifts: bfloat16 [1, 4, 768], replicated, may hold values from -3 to 3
Outputs:
- output: bfloat16 [2, 512, 16, 768], P('mp', 'dp')
- input_grad: bfloat16 [2, 512, 16, 768], P('mp', 'dp')
- attn_in_grad: float32 [1, 3, 768, 768], P(None, None, 'dp', 'mp')
- attn_out_grad: float32 [1, 768, 768], P(None, 'mp', 'dp')
- ffn_in_grad: float32 [1, 768, 3072], P(None, 'dp', 'mp')
- ffn_out_grad: float32 [1, 3072, 768], P(None, 'mp', 'dp')
- attn_bias_grad: float32 [1, 2, 768], replicated
- ffn_bias_grad: float32 [1, 3072], replicated
- norm_gain_grad: float32 [1, 2, 768], replicated
- shifts_grad: float32 [1, 4, 768], replicated
Inputs may be any that keep to these rules, and one draw needn't show every extreme that they name: `lengths`: some sequence has exactly 1024 valid tokens. `deal_order`: a permutation of the sequences; slot s is processed by data group s.
All inputs are finite; a program needn't handle non-finite values.
Results may differ from a plain program's by a relative error of at most 0.02.
Values may be sent and summed in bfloat16 or wider, within the bound.
No kernel may reach another device: no remote copies, remote signals or barrier semaphores. Data moves between devices by JAX's collectives and lax.ppermute only.
A program may use at most 128 MiB of HBM per device.

v0:
```python
import jax
import jax.numpy as jnp
from jax import lax
from jax.sharding import PartitionSpec as P

HEAD_DIM = 64
eps_norm = 1e-12
root_half = 0.7071067811865476
inv_root_two_pi = 0.3989422804014327
negative_fill = -1000000000.0


def gather_rows(rows_low):
    return lax.all_gather(rows_low, "mp", axis=0, tiled=True)


def gather_grads(rows_low):
    return lax.all_gather(rows_low, "mp", axis=0, tiled=True)


def spread_rows(make_term, row_count):
    return lax.psum_scatter(
        make_term(jnp.int32(0), row_count * lax.axis_size("mp")).astype(jnp.bfloat16),
        "mp",
        scatter_dimension=0,
        tiled=True,
    ).astype(jnp.float32)


def spread_grads(make_term, row_count):
    return lax.psum_scatter(
        make_term(jnp.int32(0), row_count * lax.axis_size("mp")).astype(jnp.bfloat16),
        "mp",
        scatter_dimension=0,
        tiled=True,
    ).astype(jnp.float32)


def fetch_weights(three_part, back_part, up_part, down_part):
    return (
        lax.all_gather(three_part, "dp", axis=1, tiled=True),
        lax.all_gather(back_part, "dp", axis=1, tiled=True),
        lax.all_gather(up_part, "dp", axis=0, tiled=True),
        lax.all_gather(down_part, "dp", axis=1, tiled=True),
    )


def fetch_again(three_part, back_part, up_part, down_part):
    return (
        lax.all_gather(three_part, "dp", axis=1, tiled=True),
        lax.all_gather(back_part, "dp", axis=1, tiled=True),
        lax.all_gather(up_part, "dp", axis=0, tiled=True),
        lax.all_gather(down_part, "dp", axis=1, tiled=True),
    )


def contract_rows(left_rows, right_rows):
    return lax.dot_general(
        left_rows, right_rows, (((0,), (0,)), ((), ())), preferred_element_type=jnp.float32
    )


def contract_cols(left_rows, right_rows):
    return lax.dot_general(
        left_rows, right_rows, (((1,), (1,)), ((), ())), preferred_element_type=jnp.float32
    )


def norm_forward(mixed_rows, gain, shift):
    center = mixed_rows - jnp.mean(mixed_rows, axis=1, keepdims=True)
    rstd_rows = lax.rsqrt(jnp.mean(center * center, axis=1, keepdims=True) + eps_norm)
    normed = center * rstd_rows
    return (normed * gain + shift, normed, rstd_rows)


def norm_backward(grad_rows, normed, rstd_rows, gain):
    scaled = grad_rows * gain
    inner = (
        scaled
        - jnp.mean(scaled, axis=1, keepdims=True)
        - normed * jnp.mean(scaled * normed, axis=1, keepdims=True)
    )
    return (rstd_rows * inner, jnp.sum(grad_rows * normed, axis=0), jnp.sum(grad_rows, axis=0))


def gelu_value(hidden_pre):
    return 0.5 * hidden_pre * (1.0 + lax.erf(hidden_pre * root_half))


def gelu_slope(hidden_pre):
    return (
        0.5 * (1.0 + lax.erf(hidden_pre * root_half))
        + hidden_pre * jnp.exp(-0.5 * hidden_pre * hidden_pre) * inv_root_two_pi
    )


def attend_forward(queries, key_rows, values, key_valid, score_scale):
    length = queries.shape[0]
    block_rows = min(512, length)
    query_blocks = queries.reshape((length // block_rows, block_rows) + queries.shape[1:])

    def one_block(query_block):
        scores = (
            jnp.einsum("qshe,kshe->shqk", query_block, key_rows, preferred_element_type=jnp.float32)
            * score_scale
        )
        scores = jnp.where(key_valid[:, None, None, :], scores, negative_fill)
        row_top = jnp.max(scores, axis=3, keepdims=True)
        exponent = jnp.exp(scores - row_top)
        row_total = jnp.sum(exponent, axis=3, keepdims=True)
        probs_low = (exponent / row_total).astype(jnp.bfloat16)
        context = jnp.einsum(
            "shqk,kshe->qshe", probs_low, values, preferred_element_type=jnp.float32
        )
        return (context.astype(jnp.bfloat16), (row_top + jnp.log(row_total))[..., 0])

    context, lse_rows = lax.map(one_block, query_blocks)
    return (context.reshape(queries.shape), lse_rows)


def attend_backward(queries, key_rows, values, grad_context, lse_rows, key_valid, score_scale):
    length = queries.shape[0]
    block_rows = min(512, length)
    block_shape = (length // block_rows, block_rows) + queries.shape[1:]

    def one_block(carry, pieces):
        grad_keys, grad_values = carry
        query_block, grad_block, lse_block = pieces
        scores = (
            jnp.einsum("qshe,kshe->shqk", query_block, key_rows, preferred_element_type=jnp.float32)
            * score_scale
        )
        scores = jnp.where(key_valid[:, None, None, :], scores, negative_fill)
        probs = jnp.exp(scores - lse_block[..., None])
        grad_values = grad_values + jnp.einsum(
            "shqk,qshe->kshe",
            probs.astype(jnp.bfloat16),
            grad_block,
            preferred_element_type=jnp.float32,
        )
        grad_probs = jnp.einsum(
            "qshe,kshe->shqk", grad_block, values, preferred_element_type=jnp.float32
        )
        inner = jnp.sum(probs * grad_probs, axis=3, keepdims=True)
        grad_scores = (probs * (grad_probs - inner) * score_scale).astype(jnp.bfloat16)
        grad_query = jnp.einsum(
            "shqk,kshe->qshe", grad_scores, key_rows, preferred_element_type=jnp.float32
        )
        grad_keys = grad_keys + jnp.einsum(
            "shqk,qshe->kshe", grad_scores, query_block, preferred_element_type=jnp.float32
        )
        return ((grad_keys, grad_values), grad_query)

    zero_rows = jnp.zeros(key_rows.shape, jnp.float32)
    pieces = (queries.reshape(block_shape), grad_context.reshape(block_shape), lse_rows)
    (grad_keys, grad_values), grad_queries = lax.scan(one_block, (zero_rows, zero_rows), pieces)
    return (grad_queries.reshape(queries.shape), grad_keys, grad_values)


def local(
    tokens,
    cotangent,
    lengths,
    deal_order,
    attn_in,
    attn_out,
    ffn_in,
    ffn_out,
    attn_bias,
    ffn_bias,
    norm_gain,
    shifts,
):
    group_count = lax.axis_size("dp")
    local_seqs = tokens.shape[2] // group_count
    dealt_tokens = jnp.take(tokens, deal_order, axis=2)
    dealt_cot = jnp.take(cotangent, deal_order, axis=2)
    arrived, arrived_cot = (
        lax.all_to_all(dealt_tokens, "dp", split_axis=2, concat_axis=1, tiled=True),
        lax.all_to_all(dealt_cot, "dp", split_axis=2, concat_axis=1, tiled=True),
    )
    half_len = arrived.shape[1]
    model_width = arrived.shape[3]
    tensor_size = lax.axis_size("mp")
    tensor_rank = lax.axis_index("mp")
    seq_len = half_len * tensor_size
    local_rows = half_len * local_seqs
    own_seqs = lax.dynamic_slice_in_dim(deal_order, lax.axis_index("dp") * local_seqs, local_seqs)
    own_lengths = jnp.take(lengths, own_seqs)
    key_valid = jnp.arange(seq_len, dtype=jnp.int32)[None, :] < own_lengths[:, None]
    head_cols = attn_in.shape[3]
    hidden_cols = ffn_in.shape[2]
    head_count = head_cols // HEAD_DIM
    score_scale = HEAD_DIM ** (-0.5)
    layers_total = norm_gain.shape[0]
    shaped = (seq_len, local_seqs, head_count, HEAD_DIM)
    flat_shape = (seq_len * local_seqs, head_cols)

    def layer_vectors(which_layer):
        bias_pair = lax.dynamic_slice_in_dim(
            attn_bias[which_layer].astype(jnp.float32), tensor_rank * head_cols, head_cols, 1
        )
        bias_up = lax.dynamic_slice_in_dim(
            ffn_bias[which_layer].astype(jnp.float32), tensor_rank * hidden_cols, hidden_cols, 0
        )
        return (
            bias_pair,
            bias_up,
            norm_gain[which_layer].astype(jnp.float32),
            shifts[which_layer].astype(jnp.float32),
        )

    hidden_rows = arrived.reshape(local_rows, model_width).astype(jnp.float32)
    weights_all = []
    which_layer = 0
    w_three, w_back, w_up, w_down = fetch_weights(
        attn_in[which_layer], attn_out[which_layer], ffn_in[which_layer], ffn_out[which_layer]
    )
    bias_pair, bias_up, gain_pair, shift_four = layer_vectors(which_layer)
    wide_rows = gather_rows(hidden_rows.astype(jnp.bfloat16))
    projected = jnp.einsum("rd,cde->cre", wide_rows, w_three, preferred_element_type=jnp.float32)
    queries = (projected[0] + bias_pair[0]).astype(jnp.bfloat16).reshape(shaped)
    key_rows = projected[1].astype(jnp.bfloat16).reshape(shaped)
    values = (projected[2] + bias_pair[1]).astype(jnp.bfloat16).reshape(shaped)
    context, lse_rows = attend_forward(queries, key_rows, values, key_valid, score_scale)
    context_rows = context.reshape(flat_shape)

    def attn_term(offset, number, context_rows=context_rows, w_back=w_back):
        return jnp.dot(context_rows, w_back, preferred_element_type=jnp.float32)

    mixed_one = hidden_rows + spread_rows(attn_term, local_rows) + shift_four[0]
    middle, mid_normed, mid_rstd = norm_forward(mixed_one, gain_pair[0], shift_four[1])
    wide_mid = gather_rows(middle.astype(jnp.bfloat16))
    hidden_pre = jnp.dot(wide_mid, w_up, preferred_element_type=jnp.float32) + bias_up
    hidden_low = gelu_value(hidden_pre).astype(jnp.bfloat16)

    def ffn_term(offset, number, hidden_low=hidden_low, w_down=w_down):
        return jnp.dot(hidden_low, w_down, preferred_element_type=jnp.float32)

    mixed_two = middle + spread_rows(ffn_term, local_rows) + shift_four[2]
    hidden_rows, out_normed, out_rstd = norm_forward(mixed_two, gain_pair[1], shift_four[3])
    saved_all = [
        (
            wide_rows,
            queries,
            key_rows,
            values,
            context,
            lse_rows,
            mid_normed,
            mid_rstd,
            wide_mid,
            hidden_pre,
            hidden_low,
            out_normed,
            out_rstd,
        )
    ]
    weights_all.append((w_three, w_back, w_up, w_down))
    grad_state = arrived_cot.reshape(local_rows, model_width).astype(jnp.float32)
    matrix_grads = [None] * layers_total
    attn_bias_parts = [None] * layers_total
    ffn_bias_parts = [None] * layers_total
    gain_parts = [None] * layers_total
    shift_parts = [None] * layers_total
    for which_layer in reversed(range(layers_total)):
        w_three, w_back, w_up, w_down = fetch_again(
            attn_in[which_layer], attn_out[which_layer], ffn_in[which_layer], ffn_out[which_layer]
        )
        bias_pair, bias_up, gain_pair, shift_four = layer_vectors(which_layer)
        (
            wide_rows,
            queries,
            key_rows,
            values,
            context,
            lse_rows,
            mid_normed,
            mid_rstd,
            wide_mid,
            hidden_pre,
            hidden_low,
            out_normed,
            out_rstd,
        ) = saved_all[which_layer]
        grad_mixed_two, grad_gain_two, grad_shift_four = norm_backward(
            grad_state, out_normed, out_rstd, gain_pair[1]
        )
        grad_down_bias = jnp.sum(grad_mixed_two, axis=0)
        grad_down_wide = gather_grads(grad_mixed_two.astype(jnp.bfloat16))
        grad_w_down = contract_rows(hidden_low, grad_down_wide)
        grad_hidden = contract_cols(grad_down_wide, w_down) * gelu_slope(hidden_pre)
        grad_up_bias = jnp.sum(grad_hidden, axis=0)
        grad_hidden_low = grad_hidden.astype(jnp.bfloat16)
        grad_w_up = contract_rows(wide_mid, grad_hidden_low)

        def up_term(offset, number, grad_hidden_low=grad_hidden_low, w_up=w_up):
            return contract_cols(grad_hidden_low, w_up)

        grad_middle = grad_mixed_two + spread_grads(up_term, local_rows)
        grad_mixed_one, grad_gain_one, grad_shift_two = norm_backward(
            grad_middle, mid_normed, mid_rstd, gain_pair[0]
        )
        grad_out_bias = jnp.sum(grad_mixed_one, axis=0)
        grad_attn_wide = gather_grads(grad_mixed_one.astype(jnp.bfloat16))
        context_rows = context.reshape(flat_shape)
        grad_w_back = contract_rows(context_rows, grad_attn_wide)
        grad_context = contract_cols(grad_attn_wide, w_back).astype(jnp.bfloat16).reshape(shaped)
        grad_queries, grad_keys, grad_values = attend_backward(
            queries, key_rows, values, grad_context, lse_rows, key_valid, score_scale
        )
        grad_queries = grad_queries.reshape(flat_shape)
        grad_keys = grad_keys.reshape(flat_shape)
        grad_values = grad_values.reshape(flat_shape)
        grad_pair = jnp.stack([jnp.sum(grad_queries, axis=0), jnp.sum(grad_values, axis=0)])
        grad_projected = jnp.stack([grad_queries, grad_keys, grad_values]).astype(jnp.bfloat16)
        grad_w_three = jnp.einsum(
            "rd,cre->cde", wide_rows, grad_projected, preferred_element_type=jnp.float32
        )

        def three_term(offset, number, grad_projected=grad_projected, w_three=w_three):
            return jnp.einsum(
                "cre,cde->rd", grad_projected, w_three, preferred_element_type=jnp.float32
            )

        grad_state = grad_mixed_one + spread_grads(three_term, local_rows)
        matrix_grads[which_layer] = (
            lax.psum_scatter(grad_w_three, "dp", scatter_dimension=1, tiled=True),
            lax.psum_scatter(grad_w_back, "dp", scatter_dimension=1, tiled=True),
            lax.psum_scatter(grad_w_up, "dp", scatter_dimension=0, tiled=True),
            lax.psum_scatter(grad_w_down, "dp", scatter_dimension=1, tiled=True),
        )
        attn_bias_parts[which_layer] = lax.dynamic_update_slice_in_dim(
            jnp.zeros((2, model_width), jnp.float32), grad_pair, tensor_rank * head_cols, 1
        )
        ffn_bias_parts[which_layer] = lax.dynamic_update_slice_in_dim(
            jnp.zeros((hidden_cols * tensor_size,), jnp.float32),
            grad_up_bias,
            tensor_rank * hidden_cols,
            0,
        )
        gain_parts[which_layer] = jnp.stack([grad_gain_one, grad_gain_two])
        shift_parts[which_layer] = jnp.stack(
            [grad_out_bias, grad_shift_two, grad_down_bias, grad_shift_four]
        )
    three_out, back_out, up_out, down_out = [
        jnp.stack([entry[member] for entry in matrix_grads]) for member in range(4)
    ]
    attn_bias_out, ffn_bias_out, gain_out, shift_out = lax.psum(
        (
            jnp.stack(attn_bias_parts),
            jnp.stack(ffn_bias_parts),
            jnp.stack(gain_parts),
            jnp.stack(shift_parts),
        ),
        ("dp", "mp"),
    )
    result_rows = hidden_rows.astype(jnp.bfloat16).reshape(1, half_len, local_seqs, model_width)
    result_grad = grad_state.astype(jnp.bfloat16).reshape(1, half_len, local_seqs, model_width)
    out_tokens, out_grad = (
        lax.all_to_all(result_rows, "dp", split_axis=1, concat_axis=2, tiled=True),
        lax.all_to_all(result_grad, "dp", split_axis=1, concat_axis=2, tiled=True),
    )
    return (
        out_tokens,
        out_grad,
        three_out,
        back_out,
        up_out,
        down_out,
        attn_bias_out,
        ffn_bias_out,
        gain_out,
        shift_out,
    )


def solution(mesh):
    placed = (
        P("mp", "dp", None, None),
        P("mp", "dp", None, None),
        P(),
        P(),
        P(None, None, "dp", "mp"),
        P(None, "mp", "dp"),
        P(None, "dp", "mp"),
        P(None, "mp", "dp"),
        P(),
        P(),
        P(),
        P(),
    )
    return jax.shard_map(
        local,
        mesh=mesh,
        in_specs=placed,
        out_specs=(
            P("mp", "dp", None, None),
            P("mp", "dp", None, None),
            P(None, None, "dp", "mp"),
            P(None, "mp", "dp"),
            P(None, "dp", "mp"),
            P(None, "mp", "dp"),
            P(),
            P(),
            P(),
            P(),
        ),
        check_vma=False,
    )
```

profile of v0, /device:TPU:0, one launch (start us, length us, event | category | flops | bytes accessed | tf_op | source)
XLA Modules:
  0.0 1211.0 jit_solution(1221424867472361412)
XLA Ops:
  12.6 29.6 %all_to_all.60 = bf16[1,32,16,768]{3,1,0,2:T(8,128)(2,1)} all-to-all(bf16[1,32,16,768]{3,1,0,2:T(8,128)(2,1)S(1)} %get-tuple-element.321), channel_id=1, replica_groups=mesh['dp'=16,'mp'=2] {'dp'}, dimensions={2} | all-to-all | bytes 1572864 | tf_op jit(solution)/shard_map/all_to_all | solution.py:179
  47.0 44.4 %all-gather.1 = bf16[1,384,768]{1,2,0:T(8,128)(2,1)} all-gather(bf16[1,384,48]{1,2,0:T(8,128)(2,1)S(1)} %copy-done.25), channel_id=3, replica_groups=mesh['dp'=16,'mp'=2] {'dp'}, dimensions={2}, use_global_device_ids=true | all-gather | bytes 626688 | tf_op jit(solution)/shard_map/all_gather | solution.py:42
  91.5 22.1 %all-gather.20.cloned.1.call-done = bf16[1,3,768,384]{3,2,1,0:T(8,128)(2,1)} async-done(((bf16[1,3,48,384]{3,2,1,0:T(8,128)(2,1)}), bf16[1,3,768,384]{3,2,1,0:T(8,128)(2,1)}) %all-gather.20.cloned.1.call-update) | async-done | bytes 1769488 | tf_op jit(solution)/shard_map/all_gather | solution.py:41
  113.6 4.0 convolution_bitcast_fusion
  119.2 2.5 squeeze.19
  123.9 18.0 %while.29 = (s32[]{:T(128)}, bf16[2,512,1,6,64]{1,4,3,2,0:T(8,128)(2,1)S(1)}, f32[2,1,6,512]{3,2,1,0:T(8,128)S(1)}, bf16[2,512,1,6,64]{1,4,3,2,0:T(8,128)(2,1)S(...) while((s32[]{:T(128)}, ...), condition=%wide.region_3.5_spmd.clone, body=%wide.region_0.4_spmd.clone.sunk | while | flops 843249664 | bytes 40231020 | solution.py:117
  125.9 3.0 fusion.175
  129.0 3.9 fusion.176
  134.9 3.0 fusion.175
  138.0 3.9 fusion.176
  147.2 6.8 reduce-scatter.8.cloned.1.call-done
  158.1 62.5 %all-gather.22.cloned.1.call-done = bf16[1,768,1536]{2,1,0:T(8,128)(2,1)} async-done(((bf16[1,48,1536]{2,1,0:T(8,128)(2,1)}), bf16[1,768,1536]{2,1,0:T(8,128)(2,1)}) %all-gather.22.cloned.1.call-update) | async-done | bytes 2359312 | tf_op jit(solution)/shard_map/all_gather | solution.py:43
  220.6 10.7 all-gather.14.cloned.1.call-done
  231.2 7.1 multiply_convert_fusion.1
  238.4 59.4 %all-gather.24.cloned.1.call-done = bf16[1,1536,768]{1,2,0:T(8,128)(2,1)} async-done(((bf16[1,1536,48]{1,2,0:T(8,128)(2,1)}), bf16[1,1536,768]{1,2,0:T(8,128)(2,1)}) %all-gather.24.cloned.1.call-update) | async-done | bytes 2359312 | tf_op jit(solution)/shard_map/all_gather | solution.py:44
  297.8 6.5 fusion.104
  304.4 25.7 %all_to_all.61 = bf16[1,32,16,768]{3,1,0,2:T(8,128)(2,1)S(1)} all-to-all(bf16[1,32,16,768]{3,1,0,2:T(8,128)(2,1)} %get-tuple-element.320), channel_id=1, replica_groups=mesh['dp'=16,'mp'=2] {'dp'}, dimensions={2} | all-to-all | bytes 1572864 | tf_op jit(solution)/shard_map/all_to_all | solution.py:180
  338.0 7.7 all-gather.16.cloned.1.call-done
  345.7 7.7 fusion.141
  355.1 3.7 fusion.101
  358.9 10.3 reduce-scatter.12.cloned.1.call-done
  369.3 3.4 multiply_reduce_fusion.1
  376.3 11.1 all-gather.18.cloned.1.call-done
  392.7 163.6 %while.30 = (s32[]{:T(128)}, f32[1024,1,6,64]{0,3,2,1:T(8,128)}, f32[1024,1,6,64]{0,3,2,1:T(8,128)}, f32[2,512,1,6,64]{1,4,3,2,0:T(8,128)}, bf16[2,512,1,6,64]{1...) while((s32[]{:T(128)}, f32[1024,1,6,64]{0,3,2,1:T(8,128)}, ...), condition=%wide.region_17.19_spmd.clone, body=%wide.region_15.18_spmd.clone.sunk | while | flops 2096636928 | bytes 199866560 | solution.py:156
  394.8 5.0 bitcast_add_fusion.5
  399.8 6.3 fusion.187
  406.1 34.3 %bitcast_add_fusion.4 = f32[1024,1,6,64]{0,3,2,1:T(8,128)} fusion(f32[1024,1,6,64]{0,3,2,1:T(8,128)} %get-tuple-element.475, f32[6,512,1024]{2,1,0:T(8,128)} %fusion.187, f32[6,512,1024]{2,1,0:T(8,128)} %copy-done, f32[6,512]{1,0:T(8,128)S(1)} %dynamic-slice_bitcast_fusion.3, pred[1024]{0:T(1024)(128)(4,1)S(1)} %compare_reduce_fusion.5, ...), kind=kOutput, calls=%fused_computation.42.clone.1 | convolution fusion | flops 438046720 | bytes 53905412 | tf_op jit(solution)/shard_map/while/body/eval_jaxpr/shqk,qshe->kshe/dot_general | solution.py:149
  440.4 33.6 %fusion.189 = f32[2,512,1,6,64]{1,4,3,2,0:T(8,128)} fusion(f32[2,512,1,6,64]{1,4,3,2,0:T(8,128)} %get-tuple-element.477, s32[]{:T(128)S(6)} %copy.127, f32[6,512,1024]{2,1,0:T(8,128)} %fusion.187, f32[6,512,1024]{2,1,0:T(8,128)} %copy-done, f32[6,512]{1,0:T(8,128)S(1)} %dynamic-slice_bitcast_fusion.3, pred[1024]{0:T(1024)(128)(4,1)S(1)} %compare_reduce_fusion.5, ...), kind=kOutput, calls=%fused_computation.44.clone.1 | convolution fusion | flops 437260288 | bytes 51939332 | tf_op jit(solution)/shard_map/while/body/eval_jaxpr/shqk,kshe->qshe/dot_general | solution.py:146
  475.9 5.9 bitcast_add_fusion.5
  481.7 6.3 fusion.187
  488.0 34.5 %bitcast_add_fusion.4 = f32[1024,1,6,64]{0,3,2,1:T(8,128)} fusion(f32[1024,1,6,64]{0,3,2,1:T(8,128)} %get-tuple-element.475, f32[6,512,1024]{2,1,0:T(8,128)} %fusion.187, f32[6,512,1024]{2,1,0:T(8,128)} %copy-done, f32[6,512]{1,0:T(8,128)S(1)} %dynamic-slice_bitcast_fusion.3, pred[1024]{0:T(1024)(128)(4,1)S(1)} %compare_reduce_fusion.5, ...), kind=kOutput, calls=%fused_computation.42.clone.1 | convolution fusion | flops 438046720 | bytes 53905412 | tf_op jit(solution)/shard_map/while/body/eval_jaxpr/shqk,qshe->kshe/dot_general | solution.py:149
  522.6 33.6 %fusion.189 = f32[2,512,1,6,64]{1,4,3,2,0:T(8,128)} fusion(f32[2,512,1,6,64]{1,4,3,2,0:T(8,128)} %get-tuple-element.477, s32[]{:T(128)S(6)} %copy.127, f32[6,512,1024]{2,1,0:T(8,128)} %fusion.187, f32[6,512,1024]{2,1,0:T(8,128)} %copy-done, f32[6,512]{1,0:T(8,128)S(1)} %dynamic-slice_bitcast_fusion.3, pred[1024]{0:T(1024)(128)(4,1)S(1)} %compare_reduce_fusion.5, ...), kind=kOutput, calls=%fused_computation.44.clone.1 | convolution fusion | flops 437260288 | bytes 51939332 | tf_op jit(solution)/shard_map/while/body/eval_jaxpr/shqk,kshe->qshe/dot_general | solution.py:146
  564.3 5.2 bitcast_convert_fusion
  569.5 4.2 convolution_bitcast_fusion.1
  573.8 4.0 copy.89
  579.0 3.5 fusion.142
  582.6 6.3 fusion.143
  590.8 6.6 fusion.118
  600.3 5.4 reduce.35
  606.8 6.9 all-to-all-start.1
  616.2 5.4 reduce.36
  622.8 22.3 %all-to-all-done.1 = bf16[16,2,12288]{2,1,0:T(2,128)(2,1)S(1)} async-done(((bf16[16,2,12288]{2,1,0:T(2,128)(2,1)}), bf16[16,2,12288]{2,1,0:T(2,128)(2,1)S(1)}, u32[]{:S(2)}, u32[]{:S(2)}) %all-to-all-start.1) | async-done | bytes 786464 | tf_op jit(solution)/shard_map/all_to_all | solution.py:361
  645.1 9.7 all-to-all-start.3
  658.8 46.7 %all-reduce.1 = (f32[1,2,768]{2,1,0:T(2,128)}, f32[1,3072]{1,0:T(1,128)}, f32[1,2,768]{2,1,0:T(2,128)}, f32[1,4,768]{2,1,0:T(4,128)}) all-reduce(f32[1,2,768]{2,1,0:T(2,128)S(1)} %fusion.130, f32[1,3072]{1,0:T(1,128)S(1)} %reshape_dynamic-update-slice_fusion, ...), channel_id=1, replica_groups=mesh['dp'=16,'mp'=2] {'dp','mp'}, use_global_device_ids=true, to_apply=%region_25.27 | all-reduce | flops 9216 | bytes 73728 | tf_op jit(solution)/shard_map/psum | solution.py:349
  705.5 85.9 %all-reduce.4.cloned.1.call-done = f32[3,768,384]{2,0,1:T(4,128)} async-done(((f32[3,768,384]{2,0,1:T(4,128)}), f32[3,768,384]{2,0,1:T(4,128)}) %all-reduce.4.cloned.1.call-update) | async-done | bytes 3538960
  795.3 124.7 %reduce-scatter.16.cloned.1.call-done = f32[384,48]{0,1:T(8,128)} async-done(((f32[384,768]{0,1:T(8,128)}), f32[384,48]{0,1:T(8,128)}) %reduce-scatter.16.cloned.1.call-update) | async-done | bytes 73744 | tf_op jit(solution)/shard_map/reduce_scatter | solution.py:329
  920.1 142.5 %reduce-scatter.20.cloned.1.call-done = f32[1536,48]{0,1:T(8,128)} async-done(((f32[1536,768]{0,1:T(8,128)}), f32[1536,48]{0,1:T(8,128)}) %reduce-scatter.20.cloned.1.call-update) | async-done | bytes 294928 | tf_op jit(solution)/shard_map/reduce_scatter | solution.py:331
  1062.6 141.7 %reduce-scatter.18.cloned.1.call-done = f32[48,1536]{1,0:T(8,128)} async-done(((f32[768,1536]{1,0:T(8,128)}), f32[48,1536]{1,0:T(8,128)}) %reduce-scatter.18.cloned.1.call-update) | async-done | bytes 294928 | tf_op jit(solution)/shard_map/reduce_scatter | solution.py:330
  (221 shorter events, 72.4 us)
Async XLA Ops:
  7.2 2.8 copy-start.17
  7.2 84.3 %all-gather.12.cloned.1.call-start = ((), (), s32[]{:S(2)}) async-start(), calls=%async_computation.11 | async-start | bytes 2359296 | tf_op jit(solution)/shard_map/all_gather | solution.py:14
  12.5 30.5 %copy-start.38 = (s32[16]{0:T(128)S(1)}, s32[16]{0:T(128)}, u32[]{:S(2)}) copy-start(s32[16]{0:T(128)} %param.21) | copy-start | bytes 196
  12.5 33.0 %copy-start.35 = (bf16[1,2,768]{2,1,0:T(2,128)(2,1)S(1)}, bf16[1,2,768]{2,1,0:T(2,128)(2,1)}, u32[]{:S(2)}) copy-start(bf16[1,2,768]{2,1,0:T(2,128)(2,1)} %param.26) | copy-start | bytes 9220
  12.5 33.2 %copy-start.39 = (s32[16]{0:T(128)S(1)}, s32[16]{0:T(128)}, u32[]{:S(2)}) copy-start(s32[16]{0:T(128)} %param.20) | copy-start | bytes 196
  12.5 34.5 %copy-start.25 = (bf16[1,384,48]{1,2,0:T(8,128)(2,1)S(1)}, bf16[1,384,48]{1,2,0:T(8,128)(2,1)}, u32[]{:S(2)}) copy-start(bf16[1,384,48]{1,2,0:T(8,128)(2,1)} %param.23) | copy-start | bytes 110596
  42.2 71.4 %all-gather.20.cloned.1.call-start = ((), (), s32[]{:S(2)}) async-start(), calls=%async_computation.22 | async-start | bytes 1880064 | tf_op jit(solution)/shard_map/all_gather | solution.py:41
  43.0 111.0 %reduce-scatter.8.cloned.1.call-start = ((), (), s32[]{:S(2)}) async-start(), calls=%async_computation.12 | async-start | bytes 2359296 | tf_op jit(solution)/shard_map/reduce_scatter | solution.py:22
  121.7 1.9 copy-start.11
  141.9 1.9 copy-start.23
  146.0 8.0 copy-start.1
  146.0 74.5 %all-gather.22.cloned.1.call-start = ((), (), s32[]{:S(2)}) async-start(), calls=%async_computation.23 | async-start | bytes 2506752 | tf_op jit(solution)/shard_map/all_gather | solution.py:43
  146.6 84.7 %all-gather.14.cloned.1.call-start = ((), (), s32[]{:S(2)}) async-start(), calls=%async_computation.13 | async-start | bytes 2359296 | tf_op jit(solution)/shard_map/all_gather | solution.py:14
  154.0 1.6 copy-start.2
  156.0 2.0 copy-start.33
  157.4 140.4 %all-gather.24.cloned.1.call-start = ((), (), s32[]{:S(2)}) async-start(), calls=%async_computation.24 | async-start | bytes 2506752 | tf_op jit(solution)/shard_map/all_gather | solution.py:44
  158.0 173.3 %reduce-scatter.10.cloned.1.call-start = ((), (), s32[]{:S(2)}) async-start(), calls=%async_computation.14 | async-start | bytes 2359296 | tf_op jit(solution)/shard_map/reduce_scatter | solution.py:22
  304.3 41.4 %all-gather.16.cloned.1.call-start = ((), (), s32[]{:S(2)}) async-start(), calls=%async_computation.15 | async-start | bytes 2359296 | tf_op jit(solution)/shard_map/all_gather | solution.py:18
  338.0 31.3 %reduce-scatter.12.cloned.1.call-start = ((), (), s32[]{:S(2)}) async-start(), calls=%async_computation.16 | async-start | bytes 2359296 | tf_op jit(solution)/shard_map/reduce_scatter | solution.py:31
  345.7 9.4 copy-start.36
  353.3 1.8 copy-start.13
  358.9 28.5 %all-gather.18.cloned.1.call-start = ((), (), s32[]{:S(2)}) async-start(), calls=%async_computation.17 | async-start | bytes 2359296 | tf_op jit(solution)/shard_map/all_gather | solution.py:18
  369.3 3.4 copy-start.10
  369.3 3.4 copy-start.12
  375.2 12.1 %copy-start.24 = (bf16[1,384,768]{1,2,0:T(8,128)(2,1)S(1)}, bf16[1,384,768]{1,2,0:T(8,128)(2,1)}, u32[]{:S(2)}) copy-start(bf16[1,384,768]{1,2,0:T(8,128)(2,1)} %all-gather.1) | copy-start | bytes 1769476
  376.2 237.5 %reduce-scatter.14.cloned.1.call-start = ((), (), s32[]{:S(2)}) async-start(), calls=%async_computation.18 | async-start | bytes 2359296 | tf_op jit(solution)/shard_map/reduce_scatter | solution.py:31
  390.0 2.7 copy-start.4
  394.8 5.0 copy-start
  475.8 5.9 copy-start
  559.3 1.7 copy-start.16
  561.5 2.8 copy-start.21
  561.5 2.8 copy-start.20
  564.3 5.2 copy-start.22
  569.5 222.0 %all-reduce.4.cloned.1.call-start = ((), (), s32[]{:S(2)}) async-start(), calls=%async_computation.25 | async-start | bytes 9437184
  577.8 4.8 copy-start.37
  577.8 342.2 %reduce-scatter.16.cloned.1.call-start = ((), (), s32[]{:S(2)}) async-start(), calls=%async_computation.19 | async-start | bytes 1253376 | tf_op jit(solution)/shard_map/reduce_scatter | solution.py:329
  582.5 480.1 %reduce-scatter.20.cloned.1.call-start = ((), (), s32[]{:S(2)}) async-start(), calls=%async_computation.21 | async-start | bytes 5013504 | tf_op jit(solution)/shard_map/reduce_scatter | solution.py:331
  588.9 1.9 copy-start.14
  588.9 615.4 %reduce-scatter.18.cloned.1.call-start = ((), (), s32[]{:S(2)}) async-start(), calls=%async_computation.20 | async-start | bytes 5013504 | tf_op jit(solution)/shard_map/reduce_scatter | solution.py:330
  605.7 8.0 copy-start.9
  606.8 38.3 %all-to-all-start.1 = ((bf16[16,2,12288]{2,1,0:T(2,128)(2,1)}), bf16[16,2,12288]{2,1,0:T(2,128)(2,1)S(1)}, u32[]{:S(2)}, u32[]{:S(2)}) async-start(bf16[16,2,12288]{2,1,0:T(2,128)(2,1)} %reshape.397), calls=%async_computation.3 | async-start | bytes 1572864 | tf_op jit(solution)/shard_map/all_to_all | solution.py:361
  621.6 33.1 %copy-start.40 = (u32[32]{0:T(128)S(1)}, u32[32]{0:T(128)}, u32[]{:S(2)}) copy-start(u32[32]{0:T(128)} %constant.142) | copy-start | bytes 388
  621.7 34.3 %copy-start.7 = (bf16[1,32,16,768]{3,1,0,2:T(8,128)(2,1)S(1)}, bf16[1,32,16,768]{3,1,0,2:T(8,128)(2,1)}, u32[]{:S(2)}) copy-start(bf16[1,32,16,768]{3,1,0,2:T(8,128)(2,1)} %copy-done.5) | copy-start | bytes 2359300
  622.8 33.4 %copy-start.26 = (f32[768]{0:T(1024)S(1)}, f32[768]{0:T(1024)}, u32[]{:S(2)}) copy-start(f32[768]{0:T(1024)} %get-tuple-element.255) | copy-start | bytes 9220
  645.1 148.1 %all-to-all-start.3 = ((bf16[16,2,12288]{2,1,0:T(2,128)(2,1)}), bf16[16,2,12288]{2,1,0:T(2,128)(2,1)S(1)}, u32[]{:S(2)}, u32[]{:S(2)}) async-start(bf16[16,2,12288]{2,1,0:T(2,128)(2,1)} %reshape.399), calls=%async_computation.7 | async-start | bytes 1572864 | tf_op jit(solution)/shard_map/all_to_all | solution.py:362
  657.0 1.5 copy-start.30
  657.0 1.5 copy-start.28
  657.0 1.6 copy-start.27
  (11 other events, 12.6 us)
Sparse Core Ops, SparseCore 0:
  42.3 7.5 all-gather.11
  52.6 60.9 all-gather.19
  146.1 7.8 reduce-scatter.7
  157.0 63.4 all-gather.21
  222.6 8.6 all-gather.13
  234.3 63.4 all-gather.23
  304.4 7.8 reduce-scatter.9
  338.1 7.5 all-gather.15
  359.0 10.2 reduce-scatter.11
  376.3 10.9 all-gather.17
  569.6 10.1 reduce-scatter.13
  585.4 205.9 all-reduce.3
  797.5 122.5 reduce-scatter.15
  926.5 136.0 reduce-scatter.19
  1068.2 136.0 reduce-scatter.17
where the time goes:
time: 1220 us; the launch traced here: 1210 us
  waiting for transfers between devices  710 us (58%)
  matrix products  234 us (19%)
  blocking collectives  147 us (12%)
  other arithmetic  42.7 us (4%)
  local copies, waits for them, and re-layouts  41.3 us (3%)
  between operations  18.2 us (1%)
  starting transfers between devices  17.6 us (1%)
    reduce_scatter x1, waiting for transfers between devices, local(): lax.psum_scatter(grad_w_down, 'dp', scatter_dimension=1, tiled=True)  143 us
    reduce_scatter x1, waiting for transfers between devices, local(): lax.psum_scatter(grad_w_up, 'dp', scatter_dimension=0, tiled=True)  142 us
    reduce_scatter x1, waiting for transfers between devices, local(): lax.psum_scatter(grad_w_back, 'dp', scatter_dimension=1, tiled=True)  125 us
    unnamed x16, waiting for transfers between devices  87.9 us
    dot_general x2, matrix products, one_block(): jnp.einsum('shqk,qshe->kshe', grad_scores, query_block, preferred_element...  68.8 us
    dot_general x2, matrix products, one_block(): jnp.einsum('shqk,kshe->qshe', grad_scores, key_rows, preferred_element_ty...  67.1 us
    all_gather x1, waiting for transfers between devices, fetch_weights(): lax.all_gather(up_part, 'dp', axis=0, tiled=True)  62.5 us
    all_gather x1, waiting for transfers between devices, fetch_weights(): lax.all_gather(down_part, 'dp', axis=1, tiled=True)  59.4 us
  transfers between devices with their start and end apart: 17, of which 13 were waited for; matrix products, arithmetic and copies ran while one was open for 5% of the time, Pallas kernels for 0%

commit v1 on v0

--- a/solution.py
+++ b/solution.py
@@ -8,6 +8,7 @@
 root_half = 0.7071067811865476
 inv_root_two_pi = 0.3989422804014327
 negative_fill = -1000000000.0
+_enter_sources_all = lambda work_x: lax.psum(lax.psum(work_x, "mp"), "dp")
 
 
 def gather_rows(rows_low):
@@ -346,14 +347,13 @@
     three_out, back_out, up_out, down_out = [
         jnp.stack([entry[member] for entry in matrix_grads]) for member in range(4)
     ]
-    attn_bias_out, ffn_bias_out, gain_out, shift_out = lax.psum(
+    attn_bias_out, ffn_bias_out, gain_out, shift_out = _enter_sources_all(
         (
             jnp.stack(attn_bias_parts),
             jnp.stack(ffn_bias_parts),
             jnp.stack(gain_parts),
             jnp.stack(shift_parts),
-        ),
-        ("dp", "mp"),
+        )
     )
     result_rows = hidden_rows.astype(jnp.bfloat16).reshape(1, half_len, local_seqs, model_width)
     result_grad = grad_state.astype(jnp.bfloat16).reshape(1, half_len, local_seqs, model_width)

time: 1220 us -> 1220 us (level)
  blocking collectives: 147 us -> 188 us
  waiting for transfers between devices: 710 us -> 669 us
    psum x1 -> x2, blocking collectives: 46.7 us -> 88.4 us  [_enter_sources_all = lambda work_x: lax.psum(lax.psum(work_x, 'mp'), 'dp')]
    unnamed x16, waiting for transfers between devices: 87.9 us -> 46.3 us
where the time goes in v1:
time: 1220 us; the launch traced here: 1210 us
  waiting for transfers between devices  669 us (55%)
  matrix products  234 us (19%)
  blocking collectives  188 us (15%)
  other arithmetic  42.7 us (4%)
  local copies, waits for them, and re-layouts  41.3 us (3%)
  between operations  18.2 us (1%)
  starting transfers between devices  17.6 us (1%)
    reduce_scatter x1, waiting for transfers between devices, local(): lax.psum_scatter(grad_w_down, 'dp', scatter_dimension=1, tiled=True)  143 us
    reduce_scatter x1, waiting for transfers between devices, local(): lax.psum_scatter(grad_w_up, 'dp', scatter_dimension=0, tiled=True)  142 us
    reduce_scatter x1, waiting for transfers between devices, local(): lax.psum_scatter(grad_w_back, 'dp', scatter_dimension=1, tiled=True)  125 us
    psum x2, blocking collectives, _enter_sources_all = lambda work_x: lax.psum(lax.psum(work_x, 'mp'), 'dp')  88.4 us
    dot_general x2, matrix products, one_block(): jnp.einsum('shqk,qshe->kshe', grad_scores, query_block, preferred_element...  68.8 us
    dot_general x2, matrix products, one_block(): jnp.einsum('shqk,kshe->qshe', grad_scores, key_rows, preferred_element_ty...  67.1 us
    all_gather x1, waiting for transfers between devices, fetch_weights(): lax.all_gather(up_part, 'dp', axis=0, tiled=True)  62.5 us
    all_gather x1, waiting for transfers between devices, fetch_weights(): lax.all_gather(down_part, 'dp', axis=1, tiled=True)  59.4 us
  transfers between devices with their start and end apart: 17, of which 13 were waited for; matrix products, arithmetic and copies ran while one was open for 5% of the time, Pallas kernels for 0%

profile of v1, /device:TPU:0, one launch (start us, length us, event | category | flops | bytes accessed | tf_op | source)
XLA Modules:
  0.0 1211.8 jit_solution(11907624497094423256)
XLA Ops:
  12.6 29.6 %all_to_all.60 = bf16[1,32,16,768]{3,1,0,2:T(8,128)(2,1)} all-to-all(bf16[1,32,16,768]{3,1,0,2:T(8,128)(2,1)S(1)} %get-tuple-element.325), channel_id=1, replica_groups=mesh['dp'=16,'mp'=2] {'dp'}, dimensions={2} | all-to-all | bytes 1572864 | tf_op jit(solution)/shard_map/all_to_all | solution.py:180
  47.0 44.4 %all-gather.1 = bf16[1,384,768]{1,2,0:T(8,128)(2,1)} all-gather(bf16[1,384,48]{1,2,0:T(8,128)(2,1)S(1)} %copy-done.25), channel_id=3, replica_groups=mesh['dp'=16,'mp'=2] {'dp'}, dimensions={2}, use_global_device_ids=true | all-gather | bytes 626688 | tf_op jit(solution)/shard_map/all_gather | solution.py:43
  91.5 22.1 %all-gather.20.cloned.1.call-done = bf16[1,3,768,384]{3,2,1,0:T(8,128)(2,1)} async-done(((bf16[1,3,48,384]{3,2,1,0:T(8,128)(2,1)}), bf16[1,3,768,384]{3,2,1,0:T(8,128)(2,1)}) %all-gather.20.cloned.1.call-update) | async-done | bytes 1769488 | tf_op jit(solution)/shard_map/all_gather | solution.py:42
  113.6 4.0 convolution_bitcast_fusion
  123.9 18.0 %while.29 = (s32[]{:T(128)}, bf16[2,512,1,6,64]{1,4,3,2,0:T(8,128)(2,1)S(1)}, f32[2,1,6,512]{3,2,1,0:T(8,128)S(1)}, bf16[2,512,1,6,64]{1,4,3,2,0:T(8,128)(2,1)S(...) while((s32[]{:T(128)}, ...), condition=%wide.region_3.5_spmd.clone, body=%wide.region_0.4_spmd.clone.sunk | while | flops 843249664 | bytes 40231020 | solution.py:118
  125.9 3.0 fusion.175
  129.0 3.9 fusion.176
  134.9 3.0 fusion.175
  138.0 3.9 fusion.176
  147.2 6.8 reduce-scatter.8.cloned.1.call-done
  158.1 62.5 %all-gather.22.cloned.1.call-done = bf16[1,768,1536]{2,1,0:T(8,128)(2,1)} async-done(((bf16[1,48,1536]{2,1,0:T(8,128)(2,1)}), bf16[1,768,1536]{2,1,0:T(8,128)(2,1)}) %all-gather.22.cloned.1.call-update) | async-done | bytes 2359312 | tf_op jit(solution)/shard_map/all_gather | solution.py:44
  220.6 10.7 all-gather.14.cloned.1.call-done
  231.2 7.1 multiply_convert_fusion.1
  238.4 59.4 %all-gather.24.cloned.1.call-done = bf16[1,1536,768]{1,2,0:T(8,128)(2,1)} async-done(((bf16[1,1536,48]{1,2,0:T(8,128)(2,1)}), bf16[1,1536,768]{1,2,0:T(8,128)(2,1)}) %all-gather.24.cloned.1.call-update) | async-done | bytes 2359312 | tf_op jit(solution)/shard_map/all_gather | solution.py:45
  297.8 6.5 fusion.104
  304.4 25.7 %all_to_all.61 = bf16[1,32,16,768]{3,1,0,2:T(8,128)(2,1)S(1)} all-to-all(bf16[1,32,16,768]{3,1,0,2:T(8,128)(2,1)} %get-tuple-element.324), channel_id=1, replica_groups=mesh['dp'=16,'mp'=2] {'dp'}, dimensions={2} | all-to-all | bytes 1572864 | tf_op jit(solution)/shard_map/all_to_all | solution.py:181
  338.0 7.7 all-gather.16.cloned.1.call-done
  345.7 7.7 fusion.141
  355.1 3.7 fusion.101
  358.9 10.3 reduce-scatter.12.cloned.1.call-done
  369.3 3.4 multiply_reduce_fusion.1
  376.3 11.1 all-gather.18.cloned.1.call-done
  392.7 163.6 %while.30 = (s32[]{:T(128)}, f32[1024,1,6,64]{0,3,2,1:T(8,128)}, f32[1024,1,6,64]{0,3,2,1:T(8,128)}, f32[2,512,1,6,64]{1,4,3,2,0:T(8,128)}, bf16[2,512,1,6,64]{1...) while((s32[]{:T(128)}, f32[1024,1,6,64]{0,3,2,1:T(8,128)}, ...), condition=%wide.region_17.19_spmd.clone, body=%wide.region_15.18_spmd.clone.sunk | while | flops 2096636928 | bytes 199866560 | solution.py:157
  394.8 5.0 bitcast_add_fusion.5
  399.8 6.3 fusion.187
  406.1 34.3 %bitcast_add_fusion.4 = f32[1024,1,6,64]{0,3,2,1:T(8,128)} fusion(f32[1024,1,6,64]{0,3,2,1:T(8,128)} %get-tuple-element.479, f32[6,512,1024]{2,1,0:T(8,128)} %fusion.187, f32[6,512,1024]{2,1,0:T(8,128)} %copy-done, f32[6,512]{1,0:T(8,128)S(1)} %dynamic-slice_bitcast_fusion.3, pred[1024]{0:T(1024)(128)(4,1)S(1)} %compare_reduce_fusion.5, ...), kind=kOutput, calls=%fused_computation.42.clone.1 | convolution fusion | flops 438046720 | bytes 53905412 | tf_op jit(solution)/shard_map/while/body/eval_jaxpr/shqk,qshe->kshe/dot_general | solution.py:150
  440.4 33.6 %fusion.189 = f32[2,512,1,6,64]{1,4,3,2,0:T(8,128)} fusion(f32[2,512,1,6,64]{1,4,3,2,0:T(8,128)} %get-tuple-element.481, s32[]{:T(128)S(6)} %copy.127, f32[6,512,1024]{2,1,0:T(8,128)} %fusion.187, f32[6,512,1024]{2,1,0:T(8,128)} %copy-done, f32[6,512]{1,0:T(8,128)S(1)} %dynamic-slice_bitcast_fusion.3, pred[1024]{0:T(1024)(128)(4,1)S(1)} %compare_reduce_fusion.5, ...), kind=kOutput, calls=%fused_computation.44.clone.1 | convolution fusion | flops 437260288 | bytes 51939332 | tf_op jit(solution)/shard_map/while/body/eval_jaxpr/shqk,kshe->qshe/dot_general | solution.py:147
  475.9 5.9 bitcast_add_fusion.5
  481.7 6.3 fusion.187
  488.0 34.5 %bitcast_add_fusion.4 = f32[1024,1,6,64]{0,3,2,1:T(8,128)} fusion(f32[1024,1,6,64]{0,3,2,1:T(8,128)} %get-tuple-element.479, f32[6,512,1024]{2,1,0:T(8,128)} %fusion.187, f32[6,512,1024]{2,1,0:T(8,128)} %copy-done, f32[6,512]{1,0:T(8,128)S(1)} %dynamic-slice_bitcast_fusion.3, pred[1024]{0:T(1024)(128)(4,1)S(1)} %compare_reduce_fusion.5, ...), kind=kOutput, calls=%fused_computation.42.clone.1 | convolution fusion | flops 438046720 | bytes 53905412 | tf_op jit(solution)/shard_map/while/body/eval_jaxpr/shqk,qshe->kshe/dot_general | solution.py:150
  522.6 33.6 %fusion.189 = f32[2,512,1,6,64]{1,4,3,2,0:T(8,128)} fusion(f32[2,512,1,6,64]{1,4,3,2,0:T(8,128)} %get-tuple-element.481, s32[]{:T(128)S(6)} %copy.127, f32[6,512,1024]{2,1,0:T(8,128)} %fusion.187, f32[6,512,1024]{2,1,0:T(8,128)} %copy-done, f32[6,512]{1,0:T(8,128)S(1)} %dynamic-slice_bitcast_fusion.3, pred[1024]{0:T(1024)(128)(4,1)S(1)} %compare_reduce_fusion.5, ...), kind=kOutput, calls=%fused_computation.44.clone.1 | convolution fusion | flops 437260288 | bytes 51939332 | tf_op jit(solution)/shard_map/while/body/eval_jaxpr/shqk,kshe->qshe/dot_general | solution.py:147
  564.3 5.2 bitcast_convert_fusion
  569.5 4.2 convolution_bitcast_fusion.1
  573.8 4.0 copy.89
  579.0 3.5 fusion.142
  582.6 6.3 fusion.143
  590.8 6.6 fusion.118
  600.3 5.4 reduce.35
  606.8 6.9 all-to-all-start.1
  616.2 5.4 reduce.36
  622.8 22.3 %all-to-all-done.1 = bf16[16,2,12288]{2,1,0:T(2,128)(2,1)S(1)} async-done(((bf16[16,2,12288]{2,1,0:T(2,128)(2,1)}), bf16[16,2,12288]{2,1,0:T(2,128)(2,1)S(1)}, u32[]{:S(2)}, u32[]{:S(2)}) %all-to-all-start.1) | async-done | bytes 786464 | tf_op jit(solution)/shard_map/all_to_all | solution.py:361
  645.1 9.7 all-to-all-start.3
  658.8 3.5 all-reduce.2
  662.3 84.9 %all-reduce.1 = (f32[1,2,768]{2,1,0:T(2,128)}, f32[1,3072]{1,0:T(1,128)}, f32[1,2,768]{2,1,0:T(2,128)}, f32[1,4,768]{2,1,0:T(4,128)}) all-reduce(f32[1,2,768]{2,1,0:T(2,128)S(1)} %get-tuple-element.305, f32[1,3072]{1,0:T(1,128)S(1)} %get-tuple-element.306, ...), channel_id=1, replica_groups=mesh['dp'=16,'mp'=2] {'dp'}, use_global_device_ids=true, to_apply=%region_26.28 | all-reduce | flops 9216 | bytes 73728 | tf_op jit(solution)/shard_map/psum | solution.py:11
  747.2 44.4 %all-reduce.5.cloned.1.call-done = f32[3,768,384]{2,0,1:T(4,128)} async-done(((f32[3,768,384]{2,0,1:T(4,128)}), f32[3,768,384]{2,0,1:T(4,128)}) %all-reduce.5.cloned.1.call-update) | async-done | bytes 3538960
  795.5 124.7 %reduce-scatter.16.cloned.1.call-done = f32[384,48]{0,1:T(8,128)} async-done(((f32[384,768]{0,1:T(8,128)}), f32[384,48]{0,1:T(8,128)}) %reduce-scatter.16.cloned.1.call-update) | async-done | bytes 73744 | tf_op jit(solution)/shard_map/reduce_scatter | solution.py:330
  920.2 143.0 %reduce-scatter.20.cloned.1.call-done = f32[1536,48]{0,1:T(8,128)} async-done(((f32[1536,768]{0,1:T(8,128)}), f32[1536,48]{0,1:T(8,128)}) %reduce-scatter.20.cloned.1.call-update) | async-done | bytes 294928 | tf_op jit(solution)/shard_map/reduce_scatter | solution.py:332
  1063.2 141.9 %reduce-scatter.18.cloned.1.call-done = f32[48,1536]{1,0:T(8,128)} async-done(((f32[768,1536]{1,0:T(8,128)}), f32[48,1536]{1,0:T(8,128)}) %reduce-scatter.18.cloned.1.call-update) | async-done | bytes 294928 | tf_op jit(solution)/shard_map/reduce_scatter | solution.py:331
  (222 shorter events, 74.9 us)
Async XLA Ops:
  7.2 2.8 copy-start.17
  7.2 84.3 %all-gather.12.cloned.1.call-start = ((), (), s32[]{:S(2)}) async-start(), calls=%async_computation.11 | async-start | bytes 2359296 | tf_op jit(solution)/shard_map/all_gather | solution.py:15
  12.5 30.5 %copy-start.38 = (s32[16]{0:T(128)S(1)}, s32[16]{0:T(128)}, u32[]{:S(2)}) copy-start(s32[16]{0:T(128)} %param.21) | copy-start | bytes 196
  12.5 33.0 %copy-start.35 = (bf16[1,2,768]{2,1,0:T(2,128)(2,1)S(1)}, bf16[1,2,768]{2,1,0:T(2,128)(2,1)}, u32[]{:S(2)}) copy-start(bf16[1,2,768]{2,1,0:T(2,128)(2,1)} %param.26) | copy-start | bytes 9220
  12.5 33.2 %copy-start.39 = (s32[16]{0:T(128)S(1)}, s32[16]{0:T(128)}, u32[]{:S(2)}) copy-start(s32[16]{0:T(128)} %param.20) | copy-start | bytes 196
  12.5 34.5 %copy-start.25 = (bf16[1,384,48]{1,2,0:T(8,128)(2,1)S(1)}, bf16[1,384,48]{1,2,0:T(8,128)(2,1)}, u32[]{:S(2)}) copy-start(bf16[1,384,48]{1,2,0:T(8,128)(2,1)} %param.23) | copy-start | bytes 110596
  42.2 71.4 %all-gather.20.cloned.1.call-start = ((), (), s32[]{:S(2)}) async-start(), calls=%async_computation.22 | async-start | bytes 1880064 | tf_op jit(solution)/shard_map/all_gather | solution.py:42
  43.0 111.0 %reduce-scatter.8.cloned.1.call-start = ((), (), s32[]{:S(2)}) async-start(), calls=%async_computation.12 | async-start | bytes 2359296 | tf_op jit(solution)/shard_map/reduce_scatter | solution.py:23
  121.7 1.9 copy-start.11
  141.9 1.9 copy-start.23
  146.0 8.0 copy-start.1
  146.0 74.5 %all-gather.22.cloned.1.call-start = ((), (), s32[]{:S(2)}) async-start(), calls=%async_computation.23 | async-start | bytes 2506752 | tf_op jit(solution)/shard_map/all_gather | solution.py:44
  146.6 84.7 %all-gather.14.cloned.1.call-start = ((), (), s32[]{:S(2)}) async-start(), calls=%async_computation.13 | async-start | bytes 2359296 | tf_op jit(solution)/shard_map/all_gather | solution.py:15
  154.0 1.6 copy-start.2
  156.0 2.0 copy-start.33
  157.4 140.4 %all-gather.24.cloned.1.call-start = ((), (), s32[]{:S(2)}) async-start(), calls=%async_computation.24 | async-start | bytes 2506752 | tf_op jit(solution)/shard_map/all_gather | solution.py:45
  158.0 173.3 %reduce-scatter.10.cloned.1.call-start = ((), (), s32[]{:S(2)}) async-start(), calls=%async_computation.14 | async-start | bytes 2359296 | tf_op jit(solution)/shard_map/reduce_scatter | solution.py:23
  304.3 41.4 %all-gather.16.cloned.1.call-start = ((), (), s32[]{:S(2)}) async-start(), calls=%async_computation.15 | async-start | bytes 2359296 | tf_op jit(solution)/shard_map/all_gather | solution.py:19
  338.0 31.3 %reduce-scatter.12.cloned.1.call-start = ((), (), s32[]{:S(2)}) async-start(), calls=%async_computation.16 | async-start | bytes 2359296 | tf_op jit(solution)/shard_map/reduce_scatter | solution.py:32
  345.7 9.4 copy-start.36
  353.3 1.8 copy-start.13
  358.9 28.5 %all-gather.18.cloned.1.call-start = ((), (), s32[]{:S(2)}) async-start(), calls=%async_computation.17 | async-start | bytes 2359296 | tf_op jit(solution)/shard_map/all_gather | solution.py:19
  369.3 3.4 copy-start.10
  369.3 3.4 copy-start.12
  375.2 12.1 %copy-start.24 = (bf16[1,384,768]{1,2,0:T(8,128)(2,1)S(1)}, bf16[1,384,768]{1,2,0:T(8,128)(2,1)}, u32[]{:S(2)}) copy-start(bf16[1,384,768]{1,2,0:T(8,128)(2,1)} %all-gather.1) | copy-start | bytes 1769476
  376.2 237.5 %reduce-scatter.14.cloned.1.call-start = ((), (), s32[]{:S(2)}) async-start(), calls=%async_computation.18 | async-start | bytes 2359296 | tf_op jit(solution)/shard_map/reduce_scatter | solution.py:32
  390.0 2.7 copy-start.4
  394.8 5.0 copy-start
  475.8 5.9 copy-start
  559.3 1.7 copy-start.16
  561.5 2.8 copy-start.21
  561.5 2.8 copy-start.20
  564.3 5.2 copy-start.22
  569.5 222.1 %all-reduce.5.cloned.1.call-start = ((), (), s32[]{:S(2)}) async-start(), calls=%async_computation.25 | async-start | bytes 9437184
  577.8 4.8 copy-start.37
  577.8 342.4 %reduce-scatter.16.cloned.1.call-start = ((), (), s32[]{:S(2)}) async-start(), calls=%async_computation.19 | async-start | bytes 1253376 | tf_op jit(solution)/shard_map/reduce_scatter | solution.py:330
  582.5 480.7 %reduce-scatter.20.cloned.1.call-start = ((), (), s32[]{:S(2)}) async-start(), calls=%async_computation.21 | async-start | bytes 5013504 | tf_op jit(solution)/shard_map/reduce_scatter | solution.py:332
  588.9 1.9 copy-start.14
  588.9 616.1 %reduce-scatter.18.cloned.1.call-start = ((), (), s32[]{:S(2)}) async-start(), calls=%async_computation.20 | async-start | bytes 5013504 | tf_op jit(solution)/shard_map/reduce_scatter | solution.py:331
  605.7 8.0 copy-start.9
  606.8 38.3 %all-to-all-start.1 = ((bf16[16,2,12288]{2,1,0:T(2,128)(2,1)}), bf16[16,2,12288]{2,1,0:T(2,128)(2,1)S(1)}, u32[]{:S(2)}, u32[]{:S(2)}) async-start(bf16[16,2,12288]{2,1,0:T(2,128)(2,1)} %reshape.397), calls=%async_computation.3 | async-start | bytes 1572864 | tf_op jit(solution)/shard_map/all_to_all | solution.py:361
  621.6 33.1 %copy-start.40 = (u32[32]{0:T(128)S(1)}, u32[32]{0:T(128)}, u32[]{:S(2)}) copy-start(u32[32]{0:T(128)} %constant.142) | copy-start | bytes 388
  621.7 34.3 %copy-start.7 = (bf16[1,32,16,768]{3,1,0,2:T(8,128)(2,1)S(1)}, bf16[1,32,16,768]{3,1,0,2:T(8,128)(2,1)}, u32[]{:S(2)}) copy-start(bf16[1,32,16,768]{3,1,0,2:T(8,128)(2,1)} %copy-done.5) | copy-start | bytes 2359300
  622.8 33.4 %copy-start.26 = (f32[768]{0:T(1024)S(1)}, f32[768]{0:T(1024)}, u32[]{:S(2)}) copy-start(f32[768]{0:T(1024)} %get-tuple-element.255) | copy-start | bytes 9220
  645.1 148.2 %all-to-all-start.3 = ((bf16[16,2,12288]{2,1,0:T(2,128)(2,1)}), bf16[16,2,12288]{2,1,0:T(2,128)(2,1)S(1)}, u32[]{:S(2)}, u32[]{:S(2)}) async-start(bf16[16,2,12288]{2,1,0:T(2,128)(2,1)} %reshape.399), calls=%async_computation.7 | async-start | bytes 1572864 | tf_op jit(solution)/shard_map/all_to_all | solution.py:362
  657.0 1.5 copy-start.30
  657.0 1.5 copy-start.28
  657.0 1.6 copy-start.27
  (11 other events, 12.6 us)
Sparse Core Ops, SparseCore 0:
  42.3 7.5 all-gather.11
  52.6 60.9 all-gather.19
  146.1 7.8 reduce-scatter.7
  157.0 63.4 all-gather.21
  222.6 8.6 all-gather.13
  234.3 63.4 all-gather.23
  304.4 7.8 reduce-scatter.9
  338.1 7.5 all-gather.15
  359.0 10.2 reduce-scatter.11
  376.3 10.9 all-gather.17
  569.6 10.1 reduce-scatter.13
  585.4 206.0 all-reduce.4
  797.6 122.5 reduce-scatter.15
  926.6 136.5 reduce-scatter.19
  1068.8 136.2 reduce-scatter.17
